TPU v7x, 256 devices: a whole 4x4x8 slice. The times are simulated.
256 devices in a mesh: node: 64 (over y, z, core), feat: 4 (over x).
Axes of the slice: x: 4, y: 4, z: 8, core: 2. Of those that a mesh axis runs over, the one named last changes fastest.
Arguments:
- features: bfloat16 [32768, 128], P('node', 'feat'), may hold values from -10 to 10
- send_rows: int32 [64, 64, 64], P('node'), may hold values from 0 to 511
- send_count: int32 [64, 64], P('node'), may hold values from 1 to 64, 2048 in all within a row
- tile_src: int32 [256, 16], P('node'), may hold values from 0 to 35
- tile_val: bfloat16 [256, 16, 128, 128], P('node'), may hold values from 0 to 0.0009765625
- labels: int32 [32768], P('node'), may hold values from 0 to 171
- w_self1: bfloat16 [128, 1024], P('feat'), may hold values from -0.5 to 0.5
- w_neigh1: bfloat16 [128, 1024], P('feat'), may hold values from -0.5 to 0.5
- w_self2: bfloat16 [1024, 172], P('feat'), may hold values from -0.5 to 0.5
- w_neigh2: bfloat16 [1024, 172], P('feat'), may hold values from -0.1875 to 0.1875
Outputs:
- mean_loss: float32 [], replicated
- grad_self1: float32 [128, 1024], P('feat')
- grad_neigh1: float32 [128, 1024], P('feat')
- grad_self2: float32 [1024, 172], P('feat')
- grad_neigh2: float32 [1024, 172], P('feat')
Inputs may be any that keep to these rules, and one draw needn't show every extreme that they name: `send_rows`: row indices within the sending partition's 512 rows. Each row of send_count sums to 2048 and holds 64 at least once. `tile_src`: block numbers of the destination partition's source rows: numbers below 4 name its own rows, the others its halo slots.
All inputs are finite; a program needn't handle non-finite values.
Results may differ from a plain program's by a relative error of at most 0.00095.
The roundings to bfloat16 on the way count: a program that leaves them out, or rounds other values in their place, can miss the bound.
Values may be sent and summed in bfloat16 or wider, within the bound.
A program may use at most 64 MiB of HBM per device.

v0:
```python
import math
import jax
import jax.numpy as jnp
from jax import lax
from jax.sharding import PartitionSpec as P


def pack_rows(own_rows, send_rows, send_count):
    slot_total = send_rows.shape[2]
    picked = jnp.take(own_rows, send_rows[0].reshape(-1), axis=0)
    picked = picked.reshape(send_rows.shape[1], slot_total, own_rows.shape[1])
    in_use = jnp.arange(slot_total, dtype=jnp.int32)[None, :] < send_count[0][:, None]
    return jnp.where(in_use[:, :, None], picked, jnp.zeros_like(picked))


def aggregate(own_rows, arrived, tile_src, tile_val):
    col_count = own_rows.shape[1]
    blocks = jnp.concatenate([own_rows, arrived], axis=0).reshape(-1, 128, col_count)
    chosen = jnp.take(blocks, tile_src, axis=0)
    summed = jnp.einsum("bkij,bkjh->bih", tile_val, chosen, preferred_element_type=jnp.float32)
    return summed.reshape(own_rows.shape[0], col_count).astype(jnp.bfloat16)


def spread_back(grads, tile_src, tile_val, src_total):
    col_count = grads.shape[1]
    per_tile = jnp.einsum(
        "bkij,bih->bkjh",
        tile_val,
        grads.reshape(-1, 128, col_count),
        preferred_element_type=jnp.float32,
    )
    one_hot = (
        tile_src.reshape(-1)[None, :] == jnp.arange(src_total // 128, dtype=jnp.int32)[:, None]
    ).astype(jnp.float32)
    landed = jnp.dot(
        one_hot,
        per_tile.reshape(one_hot.shape[1], -1),
        precision=lax.Precision.HIGHEST,
        preferred_element_type=jnp.float32,
    )
    return landed.reshape(src_total, col_count)


def cross_entropy(logits, labels, grad_scale):
    row_max = jnp.max(logits, axis=1, keepdims=True)
    shifted = logits - row_max
    total_exp = jnp.sum(jnp.exp(shifted), axis=1, keepdims=True)
    classes = jnp.arange(logits.shape[1], dtype=jnp.int32)
    target = (labels[:, None] == classes[None, :]).astype(jnp.float32)
    row_loss = jnp.log(total_exp)[:, 0] - jnp.sum(shifted * target, axis=1)
    grads = ((jnp.exp(shifted) / total_exp - target) * grad_scale).astype(jnp.bfloat16)
    return (row_loss, grads)


def shards(
    features,
    send_rows,
    send_count,
    tile_src,
    tile_val,
    labels,
    w_self1,
    w_neigh1,
    w_self2,
    w_neigh2,
):
    node_count = lax.axis_size("node")
    own_count = features.shape[0]
    slot_total = send_rows.shape[2]
    src_total = own_count + node_count * slot_total
    node_total = own_count * node_count
    grad_scale = 1.0 / math.sqrt(node_total)
    outgoing = pack_rows(features, send_rows, send_count)
    arrived = lax.all_to_all(outgoing, "node", split_axis=0, concat_axis=0, tiled=True).reshape(
        -1, features.shape[1]
    )
    agg_one = aggregate(features, arrived, tile_src, tile_val)
    partial_one = jnp.dot(features, w_self1, preferred_element_type=jnp.float32)
    partial_one = partial_one + jnp.dot(agg_one, w_neigh1, preferred_element_type=jnp.float32)
    pre_act = lax.psum_scatter(partial_one, "feat", scatter_dimension=1, tiled=True)
    activated, pullback = jax.vjp(lambda inner: jax.nn.gelu(inner, approximate=True), pre_act)
    hidden = activated.astype(jnp.bfloat16)
    unit_count = hidden.shape[1]
    outgoing_two = pack_rows(hidden, send_rows, send_count)
    arrived_two = lax.all_to_all(
        outgoing_two, "node", split_axis=0, concat_axis=0, tiled=True
    ).reshape(-1, unit_count)
    agg_two = aggregate(hidden, arrived_two, tile_src, tile_val)
    partial_two = jnp.dot(hidden, w_self2, preferred_element_type=jnp.float32)
    partial_two = partial_two + jnp.dot(agg_two, w_neigh2, preferred_element_type=jnp.float32)
    logits = lax.psum(partial_two, "feat")
    row_loss, dlogits = cross_entropy(logits, labels, grad_scale)
    mean_loss = lax.psum(jnp.sum(row_loss), "node") / node_total
    grad_pair = lax.psum(
        (
            jnp.einsum("nh,nc->hc", hidden, dlogits, preferred_element_type=jnp.float32),
            jnp.einsum("nh,nc->hc", agg_two, dlogits, preferred_element_type=jnp.float32),
        ),
        "node",
    )
    back_grad = jnp.einsum(
        "nc,hc->nh", dlogits, w_neigh2, preferred_element_type=jnp.float32
    ).astype(jnp.bfloat16)
    direct = jnp.einsum("nc,hc->nh", dlogits, w_self2, preferred_element_type=jnp.float32)
    landed = spread_back(back_grad, tile_src, tile_val, src_total)
    halo_back = landed[own_count:].reshape(node_count, slot_total, unit_count)
    returned = lax.all_to_all(
        halo_back.astype(jnp.bfloat16), "node", split_axis=0, concat_axis=0, tiled=True
    ).astype(halo_back.dtype)
    in_use = jnp.arange(slot_total, dtype=jnp.int32)[None, :] < send_count[0][:, None]
    returned = jnp.where(in_use[:, :, None], returned, jnp.zeros_like(returned))
    back_rows = jax.ops.segment_sum(
        returned.reshape(-1, unit_count), send_rows[0].reshape(-1), num_segments=own_count
    )
    back_hidden = direct + landed[:own_count] + back_rows
    pre_grad = pullback(back_hidden)[0].astype(jnp.bfloat16)
    shard_piece = lax.all_gather(pre_grad, "feat", axis=1, tiled=True)
    local_grads = jnp.stack(
        [
            jnp.einsum("nf,nh->fh", features, shard_piece, preferred_element_type=jnp.float32),
            jnp.einsum("nf,nh->fh", agg_one, shard_piece, preferred_element_type=jnp.float32),
        ]
    )
    summed = lax.psum(local_grads, "node")
    return (mean_loss, summed[0], summed[1], grad_pair[0], grad_pair[1])


def solution(mesh):
    in_specs = (
        P("node", "feat"),
        P("node", None, None),
        P("node", None),
        P("node", None),
        P("node", None, None, None),
        P("node"),
        P("feat", None),
        P("feat", None),
        P("feat", None),
        P("feat", None),
    )
    out_specs = (P(), P("feat", None), P("feat", None), P("feat", None), P("feat", None))
    return jax.shard_map(shards, mesh=mesh, in_specs=in_specs, out_specs=out_specs, check_vma=False)
```

profile of v0, /device:TPU:2, one launch (start us, length us, event | category | flops | bytes accessed | tf_op | source)
XLA Modules:
  0.0 571.0 jit_solution(3139560621322994043)
XLA Ops:
  7.2 1.0 reshape_squeeze.7
  8.2 0.9 iota_compare_fusion.1
  9.1 0.9 copy.35
  10.0 12.1 %gather_fusion = bf16[4096,32]{1,0:T(8,128)(2,1)S(1)} fusion(bf16[512,32]{1,0:T(8,128)(2,1)S(1)} %copy.35, s32[4096]{0:T(1024)S(1)} %broadcast_clamp_fusion), kind=kCustom, calls=%fused_computation | custom fusion | bytes 540672 | tf_op jit(solution)/shard_map/jit(_take)/gather | solution.py:10
  22.1 1.1 copy.36
  23.3 1.2 fusion.30
  24.4 1.0 reshape.178
  25.4 12.1 %all-to-all-start = ((bf16[64,2,1024]{2,1,0:T(2,128)(2,1)}), bf16[64,2,1024]{2,1,0:T(2,128)(2,1)S(1)}, u32[]{:S(2)}, u32[]{:S(2)}) async-start(bf16[64,2,1024]{2,1,0:T(2,128)(2,1)} %reshape.178), calls=%async_computation | async-start | bytes 524288 | tf_op jit(solution)/shard_map/all_to_all | solution.py:74
  37.5 0.0 reduce-scatter.2.cloned.1.call-start
  37.6 0.1 reshape.140
  37.7 1.8 fusion.31
  39.5 10.0 %all-to-all-done = bf16[64,2,1024]{2,1,0:T(2,128)(2,1)S(1)} async-done(((bf16[64,2,1024]{2,1,0:T(2,128)(2,1)}), bf16[64,2,1024]{2,1,0:T(2,128)(2,1)S(1)}, u32[]{:S(2)}, u32[]{:S(2)}) %all-to-all-start) | async-done | bytes 262176 | tf_op jit(solution)/shard_map/all_to_all | solution.py:74
  49.5 0.3 reshape.179
  49.9 0.2 copy.37
  50.1 0.5 reshape.123
  50.6 0.1 copy_bitcast_fusion
  50.6 0.7 gather_fusion.1
  51.3 0.8 fusion.11
  52.1 0.7 copy-done.3
  52.9 1.8 convolution_add_fusion
  54.7 28.0 %reduce-scatter.2.cloned.1.call-done = f32[512,256]{1,0:T(8,128)} async-done(((f32[512,1024]{1,0:T(8,128)}), f32[512,256]{1,0:T(8,128)}) %reduce-scatter.2.cloned.1.call-update) | async-done | bytes 524304 | tf_op jit(solution)/shard_map/reduce_scatter | solution.py:80
  82.7 1.2 multiply_convert_fusion
  83.9 16.9 %gather_fusion.2 = bf16[4096,256]{1,0:T(8,128)(2,1)} fusion(bf16[512,256]{1,0:T(8,128)(2,1)S(1)} %multiply_convert_fusion, s32[4096]{0:T(1024)S(1)} %broadcast_clamp_fusion), kind=kCustom, calls=%fused_computation.2 | custom fusion | bytes 4210688 | tf_op jit(solution)/shard_map/jit(_take)/gather | solution.py:10
  100.8 4.4 select_select_fusion
  105.2 10.9 %all-to-all-start.1 = ((bf16[64,64,256]{2,1,0:T(8,128)(2,1)}), bf16[64,64,256]{2,1,0:T(8,128)(2,1)}, u32[]{:S(2)}, u32[]{:S(2)}) async-start(bf16[64,64,256]{2,1,0:T(8,128)(2,1)} %select_select_fusion), calls=%async_computation.2 | async-start | bytes 4194304 | tf_op jit(solution)/shard_map/all_to_all | solution.py:85
  116.1 0.2 fusion.32
  116.4 50.7 %all-to-all-done.1 = bf16[64,64,256]{2,1,0:T(8,128)(2,1)} async-done(((bf16[64,64,256]{2,1,0:T(8,128)(2,1)}), bf16[64,64,256]{2,1,0:T(8,128)(2,1)}, u32[]{:S(2)}, u32[]{:S(2)}) %all-to-all-start.1) | async-done | bytes 2097184 | tf_op jit(solution)/shard_map/all_to_all | solution.py:85
  167.1 3.2 pad_maximum_fusion
  170.3 4.4 gather_fusion.3
  174.7 3.2 fusion.7
  178.0 1.0 convolution_add_fusion.2
  179.0 0.1 eq.31
  179.0 42.6 %all-reduce.4.cloned.1.call-done = f32[512,172]{0,1:T(8,128)} async-done(((f32[512,172]{0,1:T(8,128)}), f32[512,172]{0,1:T(8,128)}) %all-reduce.4.cloned.1.call-update) | async-done | bytes 352272 | tf_op jit(solution)/shard_map/psum | solution.py:91
  221.7 1.0 reduce_max.9
  222.7 1.1 exponential_reduce_fusion
  223.8 1.1 multiply_convert_fusion.1
  224.9 0.3 convolution_convert_fusion
  225.2 4.5 convolution_bitcast_fusion
  229.7 8.7 %copy.41 = f32[4,16,128,256]{3,2,1,0:T(8,128)} copy(f32[4,16,128,256]{2,3,1,0:T(8,128)} %convolution_bitcast_fusion) | data formatting | bytes 16777216 | tf_op jit(solution)/shard_map/bkij,bih->bkjh/dot_general | solution.py:26
  238.4 8.1 %copy.49 = f32[8,8,128,256]{3,1,2,0:T(8,128)S(1)} copy(f32[8,8,128,256]{3,2,1,0:T(8,128)} %bitcast.90) | data formatting | bytes 16777216
  246.5 4.3 fusion.26
  250.8 2.3 copy-done.2
  253.1 0.3 slice.37
  253.4 2.4 convert_element_type.51
  255.9 10.9 %all-to-all-start.2 = ((bf16[64,64,256]{2,1,0:T(8,128)(2,1)}), bf16[64,64,256]{2,1,0:T(8,128)(2,1)}, u32[]{:S(2)}, u32[]{:S(2)}) async-start(bf16[64,64,256]{2,1,0:T(8,128)(2,1)} %convert_element_type.51), calls=%async_computation.3 | async-start | bytes 4194304 | tf_op jit(solution)/shard_map/all_to_all | solution.py:107
  266.8 0.1 reshape.164
  266.9 0.4 slice.18
  267.2 0.3 convolution_add_fusion.1
  267.5 50.3 %all-to-all-done.2 = bf16[64,64,256]{2,1,0:T(8,128)(2,1)} async-done(((bf16[64,64,256]{2,1,0:T(8,128)(2,1)}), bf16[64,64,256]{2,1,0:T(8,128)(2,1)}, u32[]{:S(2)}, u32[]{:S(2)}) %all-to-all-start.2) | async-done | bytes 2097184 | tf_op jit(solution)/shard_map/all_to_all | solution.py:107
  317.8 3.5 convert_select_fusion
  321.3 23.3 %scatter_fusion = f32[512,256]{1,0:T(8,128)S(1)} fusion(f32[512,256]{1,0:T(8,128)S(1)} %convolution_add_fusion.1, s32[4096]{0:T(1024)S(1)} %reshape.164, f32[4096,256]{1,0:T(8,128)} %bitcast.92), kind=kCustom, calls=%fused_computation.4 | custom fusion | flops 1048576 | bytes 12599296 | tf_op jit(solution)/shard_map/scatter-add | solution.py:112
  344.6 1.1 fusion.18
  345.7 0.9 fusion.34
  346.6 0.9 fusion.33
  347.5 23.0 %all-gather.2.cloned.1.call-done = bf16[512,1024]{1,0:T(8,128)(2,1)} async-done(((bf16[512,256]{1,0:T(8,128)(2,1)}), bf16[512,1024]{1,0:T(8,128)(2,1)}) %all-gather.2.cloned.1.call-update) | async-done | bytes 1048592 | tf_op jit(solution)/shard_map/all_gather | solution.py:117
  370.5 1.7 convolution_bitcast_fusion.2
  372.2 1.5 convolution_bitcast_fusion.1
  373.7 0.7 pad_maximum_fusion.1
  374.4 0.6 subtract_reduce_fusion
  375.0 128.7 %psum.36 = f32[]{:T(128)} all-reduce(f32[]{:T(128)} %subtract_reduce_fusion), channel_id=1, replica_groups=mesh['node'=64,'feat'=4] {'node'}, use_global_device_ids=true, to_apply=%region_6.7 | all-reduce | flops 1 | bytes 8 | tf_op jit(solution)/shard_map/psum | solution.py:93
  504.4 54.0 %all-reduce.6.cloned.1.call-done = (f32[2,32,1024]{2,1,0:T(8,128)}, f32[256,172]{0,1:T(8,128)}, f32[256,172]{0,1:T(8,128)}) async-done(((f32[2,32,1024]{2,1,0:T(8,128)}, f32[256,172]{0,1:T(8,128)}, f32[256,172]{0,1:T(8,128)}), (f32[2,32,1024]{2,1,0:T(8,128)}, f32[256,172]{0,1:T(8,128)}, f32[256,172]{0,1:T(8,128)})) %all-reduce.6.cloned.1.call-update) | async-done | bytes 614416 | tf_op jit(solution)/shard_map/psum | solution.py:124
  558.4 1.7 slice_bitcast_fusion
  560.1 1.6 copy.64
  561.7 1.6 copy.65
  (38 shorter events, 0.3 us)
Async XLA Ops:
  7.2 44.1 %copy-start = (bf16[4,16,128,128]{3,2,1,0:T(8,128)(2,1)S(1)}, bf16[4,16,128,128]{3,2,1,0:T(8,128)(2,1)}, u32[]{:S(2)}) copy-start(bf16[4,16,128,128]{3,2,1,0:T(8,128)(2,1)} %param.14) | copy-start | bytes 6291460
  22.1 15.5 %copy-start.11 = (s32[4,16]{1,0:T(4,128)S(1)}, s32[4,16]{1,0:T(4,128)}, u32[]{:S(2)}) copy-start(s32[4,16]{1,0:T(4,128)} %param.13) | copy-start | bytes 772
  22.1 15.6 %copy-start.5 = (bf16[512,32]{0,1:T(8,128)(2,1)S(1)}, bf16[512,32]{0,1:T(8,128)(2,1)}, u32[]{:S(2)}) copy-start(bf16[512,32]{0,1:T(8,128)(2,1)} %param.10) | copy-start | bytes 98308
  22.1 15.6 %copy-start.10 = (bf16[32,1024]{1,0:T(8,128)(2,1)S(1)}, bf16[32,1024]{1,0:T(8,128)(2,1)}, u32[]{:S(2)}) copy-start(bf16[32,1024]{1,0:T(8,128)(2,1)} %param.16) | copy-start | bytes 196612
  25.4 24.1 %all-to-all-start = ((bf16[64,2,1024]{2,1,0:T(2,128)(2,1)}), bf16[64,2,1024]{2,1,0:T(2,128)(2,1)S(1)}, u32[]{:S(2)}, u32[]{:S(2)}) async-start(bf16[64,2,1024]{2,1,0:T(2,128)(2,1)} %reshape.178), calls=%async_computation | async-start | bytes 524288 | tf_op jit(solution)/shard_map/all_to_all | solution.py:74
  37.5 45.1 %reduce-scatter.2.cloned.1.call-start = ((), (), s32[]{:S(2)}) async-start(), calls=%async_computation.4 | async-start | bytes 2621440 | tf_op jit(solution)/shard_map/reduce_scatter | solution.py:80
  51.3 1.6 copy-start.3
  51.3 1.6 copy-start.9
  105.2 10.9 %copy-start.7 = (bf16[256,172]{0,1:T(8,128)(2,1)S(1)}, bf16[256,172]{0,1:T(8,128)(2,1)}, u32[]{:S(2)}) copy-start(bf16[256,172]{0,1:T(8,128)(2,1)} %param.18) | copy-start | bytes 264196
  105.2 61.9 %all-to-all-start.1 = ((bf16[64,64,256]{2,1,0:T(8,128)(2,1)}), bf16[64,64,256]{2,1,0:T(8,128)(2,1)}, u32[]{:S(2)}, u32[]{:S(2)}) async-start(bf16[64,64,256]{2,1,0:T(8,128)(2,1)} %select_select_fusion), calls=%async_computation.2 | async-start | bytes 4194304 | tf_op jit(solution)/shard_map/all_to_all | solution.py:85
  116.1 105.6 %all-reduce.4.cloned.1.call-start = ((), (), s32[]{:S(2)}) async-start(), calls=%async_computation.5 | async-start | bytes 720896 | tf_op jit(solution)/shard_map/psum | solution.py:91
  174.7 3.2 copy-start.6
  174.7 48.0 %copy-start.12 = (s32[512]{0:T(512)S(1)}, s32[512]{0:T(512)}, u32[]{:S(2)}) copy-start(s32[512]{0:T(512)} %param.15) | copy-start | bytes 6148
  250.8 2.3 copy-start.2
  255.9 10.9 %copy-start.8 = (s32[1,64,64]{2,1,0:T(8,128)S(1)}, s32[1,64,64]{2,1,0:T(8,128)}, u32[]{:S(2)}) copy-start(s32[1,64,64]{2,1,0:T(8,128)} %param.11) | copy-start | bytes 49156
  255.9 11.0 %slice-start = ((f32[36,32768]{1,0:T(8,128)}), f32[4,32768]{1,0:T(4,128)S(1)}, s32[]{:S(2)}) async-start(f32[36,32768]{1,0:T(8,128)} %copy-done.2), calls=%async_computation.8 | async-start | bytes 1048576 | tf_op jit(solution)/shard_map/slice | solution.py:115
  255.9 61.9 %all-to-all-start.2 = ((bf16[64,64,256]{2,1,0:T(8,128)(2,1)}), bf16[64,64,256]{2,1,0:T(8,128)(2,1)}, u32[]{:S(2)}, u32[]{:S(2)}) async-start(bf16[64,64,256]{2,1,0:T(8,128)(2,1)} %convert_element_type.51), calls=%async_computation.3 | async-start | bytes 4194304 | tf_op jit(solution)/shard_map/all_to_all | solution.py:107
  266.7 103.8 %all-gather.2.cloned.1.call-start = ((), (), s32[]{:S(2)}) async-start(), calls=%async_computation.6 | async-start | bytes 1310720 | tf_op jit(solution)/shard_map/all_gather | solution.py:117
  321.3 23.3 %copy-start.4 = (f32[512,256]{1,0:T(8,128)S(1)}, f32[512,256]{1,0:T(8,128)}, u32[]{:S(2)}) copy-start(f32[512,256]{1,0:T(8,128)} %reduce-scatter.2.cloned.1.call-done) | copy-start | bytes 1572868
  345.7 212.8 %all-reduce.6.cloned.1.call-start = ((), (), s32[]{:S(2)}) async-start(), calls=%async_computation.7 | async-start | bytes 1245184 | tf_op jit(solution)/shard_map/psum | solution.py:124
  370.5 192.8 %copy-start.1 = (bf16[4,16,128,128]{3,2,1,0:T(8,128)(2,1)S(1)}, bf16[4,16,128,128]{3,2,1,0:T(8,128)(2,1)}, u32[]{:S(2)}) copy-start(bf16[4,16,128,128]{3,2,1,0:T(8,128)(2,1)} %param.14) | copy-start | bytes 6291460
Sparse Core Ops, SparseCore 0:
  54.8 27.8 reduce-scatter.1
  179.1 42.5 all-reduce.3
  345.8 24.6 all-gather.1
  375.2 183.2 all-reduce.5
where the time goes:
time: 572 us; the launch traced here: 571 us
  waiting for transfers between devices  259 us (45%)
  blocking collectives  129 us (23%)
  local copies, waits for them, and re-layouts  67.3 us (12%)
  other arithmetic  43.3 us (8%)
  starting transfers between devices  34 us (6%)
  matrix products  23.1 us (4%)
  between operations  15.8 us (3%)
    psum x1, blocking collectives, shards(): mean_loss = lax.psum(jnp.sum(row_loss), 'node') / node_total  129 us
    psum x1, waiting for transfers between devices, shards(): summed = lax.psum(local_grads, 'node')  54 us
    all_to_all x1, waiting for transfers between devices, shards(): lax.all_to_all(outgoing_two, 'node', split_axis=0, concat_axis=0, tiled=T...  50.7 us
    all_to_all x1, waiting for transfers between devices, shards(): lax.all_to_all(halo_back.astype(jnp.bfloat16), 'node', split_axis=0, conc...  50.3 us
    psum x1, waiting for transfers between devices, shards(): logits = lax.psum(partial_two, 'feat')  42.6 us
    gather x3, local copies, waits for them, and re-layouts, pack_rows(): picked = jnp.take(own_rows, send_rows[0].reshape(-1), axis=0)  30.2 us
    reduce_scatter x1, waiting for transfers between devices, shards(): lax.psum_scatter(partial_one, 'feat', scatter_dimension=1, tiled=True)  28 us
    scatter-add x1, other arithmetic, shards(): jax.ops.segment_sum(returned.reshape(-1, unit_count), send_rows[0].reshap...  23.3 us
  transfers between devices with their start and end apart: 7, of which 7 were waited for; matrix products, arithmetic and copies ran while one was open for 1% of the time, Pallas kernels for 0%

commit v1 on v0

--- a/solution.py
+++ b/solution.py
@@ -1,8 +1,28 @@
+import functools
 import math
 import jax
 import jax.numpy as jnp
 from jax import lax
 from jax.sharding import PartitionSpec as P
+
+
+def put_seats_all(array_here, bus_axis, pos_dim):
+    axis_n = lax.axis_size(bus_axis)
+    chunks = list(map(lambda j0: (j0, (j0 + 1) % axis_n), range(axis_n)))
+    ledger = list(map(lambda j0: (j0, (j0 - 1) % axis_n), range(axis_n)))
+    then, base_arr = ([array_here], [array_here])
+    for _ in range(axis_n // 2):
+        then.append(lax.ppermute(then[-1], bus_axis, chunks))
+    for _ in range((axis_n - 1) // 2):
+        base_arr.append(lax.ppermute(base_arr[-1], bus_axis, ledger))
+    return jnp.roll(
+        jnp.concatenate([*then[::-1], *base_arr[1:]], pos_dim),
+        (lax.axis_index(bus_axis) - axis_n // 2) * array_here.shape[pos_dim],
+        pos_dim,
+    )
+
+
+levels_all_feed = functools.partial(put_seats_all, bus_axis="feat", pos_dim=1)
 
 
 def pack_rows(own_rows, send_rows, send_count):
@@ -114,7 +134,7 @@
     )
     back_hidden = direct + landed[:own_count] + back_rows
     pre_grad = pullback(back_hidden)[0].astype(jnp.bfloat16)
-    shard_piece = lax.all_gather(pre_grad, "feat", axis=1, tiled=True)
+    shard_piece = levels_all_feed(pre_grad)
     local_grads = jnp.stack(
         [
             jnp.einsum("nf,nh->fh", features, shard_piece, preferred_element_type=jnp.float32),

time: 572 us -> 560 us (0.979)
  waiting for transfers between devices: 259 us -> 249 us
    all_gather x1 -> x0, waiting for transfers between devices: 23 us -> none  [shards(): shard_piece = lax.all_gather(pre_grad, 'feat', axis=1, tiled=True)]
    ppermute x0 -> x3, waiting for transfers between devices: none -> 12.6 us  [the longest x2 10.6 us: put_seats_all(): then.append(lax.ppermute(then[-1], bus_axis, chunks))]
    unnamed x32 -> x39, local copies, waits for them, and re-layouts: 16.6 us -> 16.8 us
  transfers between devices with their start and end apart: 7 -> 9, of which waited for: 7 -> 9; matrix products, arithmetic and copies ran while one was open for 1% -> 1% of each run, Pallas kernels for 0% -> 0%
where the time goes in v1:
time: 560 us; the launch traced here: 559 us
  waiting for transfers between devices  249 us (44%)
  blocking collectives  125 us (22%)
  local copies, waits for them, and re-layouts  67.5 us (12%)
  other arithmetic  42.6 us (8%)
  starting transfers between devices  38.5 us (7%)
  matrix products  20.5 us (4%)
  between operations  15.9 us (3%)
    psum x1, blocking collectives, shards(): mean_loss = lax.psum(jnp.sum(row_loss), 'node') / node_total  125 us
    psum x1, waiting for transfers between devices, shards(): summed = lax.psum(local_grads, 'node')  54.8 us
    all_to_all x1, waiting for transfers between devices, shards(): lax.all_to_all(outgoing_two, 'node', split_axis=0, concat_axis=0, tiled=T...  50.7 us
    all_to_all x1, waiting for transfers between devices, shards(): lax.all_to_all(halo_back.astype(jnp.bfloat16), 'node', split_axis=0, conc...  50.3 us
    psum x1, waiting for transfers between devices, shards(): logits = lax.psum(partial_two, 'feat')  42.6 us
    gather x3, local copies, waits for them, and re-layouts, pack_rows(): picked = jnp.take(own_rows, send_rows[0].reshape(-1), axis=0)  30.2 us
    reduce_scatter x1, waiting for transfers between devices, shards(): lax.psum_scatter(partial_one, 'feat', scatter_dimension=1, tiled=True)  28 us
    scatter-add x1, other arithmetic, shards(): jax.ops.segment_sum(returned.reshape(-1, unit_count), send_rows[0].reshap...  23.3 us
  transfers between devices with their start and end apart: 9, of which 9 were waited for; matrix products, arithmetic and copies ran while one was open for 1% of the time, Pallas kernels for 0%

profile of v1, /device:TPU:2, one launch (start us, length us, event | category | flops | bytes accessed | tf_op | source)
XLA Modules:
  0.0 559.0 jit_solution(7393468102264012531)
XLA Ops:
  7.2 1.0 reshape_squeeze.7
  8.2 0.9 iota_compare_fusion.1
  9.1 0.9 copy.35
  10.0 12.1 %gather_fusion = bf16[4096,32]{1,0:T(8,128)(2,1)S(1)} fusion(bf16[512,32]{1,0:T(8,128)(2,1)S(1)} %copy.35, s32[4096]{0:T(1024)S(1)} %broadcast_clamp_fusion), kind=kCustom, calls=%fused_computation | custom fusion | bytes 540672 | tf_op jit(solution)/shard_map/jit(_take)/gather | solution.py:30
  22.1 1.1 copy.36
  23.3 1.2 fusion.34
  24.4 1.0 reshape.178
  25.4 12.1 %all-to-all-start = ((bf16[64,2,1024]{2,1,0:T(2,128)(2,1)}), bf16[64,2,1024]{2,1,0:T(2,128)(2,1)S(1)}, u32[]{:S(2)}, u32[]{:S(2)}) async-start(bf16[64,2,1024]{2,1,0:T(2,128)(2,1)} %reshape.178), calls=%async_computation | async-start | bytes 524288 | tf_op jit(solution)/shard_map/all_to_all | solution.py:94
  37.7 1.8 fusion.35
  39.5 10.0 %all-to-all-done = bf16[64,2,1024]{2,1,0:T(2,128)(2,1)S(1)} async-done(((bf16[64,2,1024]{2,1,0:T(2,128)(2,1)}), bf16[64,2,1024]{2,1,0:T(2,128)(2,1)S(1)}, u32[]{:S(2)}, u32[]{:S(2)}) %all-to-all-start) | async-done | bytes 262176 | tf_op jit(solution)/shard_map/all_to_all | solution.py:94
  49.5 0.3 reshape.179
  49.9 0.2 copy.37
  50.1 0.5 reshape.123
  50.6 0.7 gather_fusion.1
  51.3 0.8 fusion.11
  52.1 0.7 copy-done.3
  52.9 1.8 convolution_add_fusion
  54.7 28.0 %reduce-scatter.2.cloned.1.call-done = f32[512,256]{1,0:T(8,128)} async-done(((f32[512,1024]{1,0:T(8,128)}), f32[512,256]{1,0:T(8,128)}) %reduce-scatter.2.cloned.1.call-update) | async-done | bytes 524304 | tf_op jit(solution)/shard_map/reduce_scatter | solution.py:100
  82.7 1.2 multiply_convert_fusion
  83.9 16.9 %gather_fusion.2 = bf16[4096,256]{1,0:T(8,128)(2,1)} fusion(bf16[512,256]{1,0:T(8,128)(2,1)S(1)} %multiply_convert_fusion, s32[4096]{0:T(1024)S(1)} %broadcast_clamp_fusion), kind=kCustom, calls=%fused_computation.2 | custom fusion | bytes 4210688 | tf_op jit(solution)/shard_map/jit(_take)/gather | solution.py:30
  100.8 4.4 select_select_fusion
  105.2 10.9 %all-to-all-start.1 = ((bf16[64,64,256]{2,1,0:T(8,128)(2,1)}), bf16[64,64,256]{2,1,0:T(8,128)(2,1)}, u32[]{:S(2)}, u32[]{:S(2)}) async-start(bf16[64,64,256]{2,1,0:T(8,128)(2,1)} %select_select_fusion), calls=%async_computation.2 | async-start | bytes 4194304 | tf_op jit(solution)/shard_map/all_to_all | solution.py:105
  116.1 0.2 fusion.36
  116.4 50.7 %all-to-all-done.1 = bf16[64,64,256]{2,1,0:T(8,128)(2,1)} async-done(((bf16[64,64,256]{2,1,0:T(8,128)(2,1)}), bf16[64,64,256]{2,1,0:T(8,128)(2,1)}, u32[]{:S(2)}, u32[]{:S(2)}) %all-to-all-start.1) | async-done | bytes 2097184 | tf_op jit(solution)/shard_map/all_to_all | solution.py:105
  167.1 3.2 pad_maximum_fusion
  170.3 4.4 gather_fusion.3
  174.7 3.2 fusion.7
  178.0 1.0 convolution_add_fusion.2
  179.0 42.6 %all-reduce.4.cloned.1.call-done = f32[512,172]{0,1:T(8,128)} async-done(((f32[512,172]{0,1:T(8,128)}), f32[512,172]{0,1:T(8,128)}) %all-reduce.4.cloned.1.call-update) | async-done | bytes 352272 | tf_op jit(solution)/shard_map/psum | solution.py:111
  221.7 1.0 reduce_max.9
  222.7 1.1 exponential_reduce_fusion
  223.8 1.1 multiply_convert_fusion.1
  224.9 0.3 convolution_convert_fusion
  225.2 4.5 convolution_bitcast_fusion
  229.7 8.7 %copy.41 = f32[4,16,128,256]{3,2,1,0:T(8,128)} copy(f32[4,16,128,256]{2,3,1,0:T(8,128)} %convolution_bitcast_fusion) | data formatting | bytes 16777216 | tf_op jit(solution)/shard_map/bkij,bih->bkjh/dot_general | solution.py:46
  238.4 8.1 %copy.49 = f32[8,8,128,256]{3,1,2,0:T(8,128)S(1)} copy(f32[8,8,128,256]{3,2,1,0:T(8,128)} %bitcast.88) | data formatting | bytes 16777216
  246.5 4.3 fusion.28
  250.8 2.3 copy-done.2
  253.1 0.3 slice.37
  253.4 2.4 convert_element_type.51
  255.9 10.9 %all-to-all-start.2 = ((bf16[64,64,256]{2,1,0:T(8,128)(2,1)}), bf16[64,64,256]{2,1,0:T(8,128)(2,1)}, u32[]{:S(2)}, u32[]{:S(2)}) async-start(bf16[64,64,256]{2,1,0:T(8,128)(2,1)} %convert_element_type.51), calls=%async_computation.3 | async-start | bytes 4194304 | tf_op jit(solution)/shard_map/all_to_all | solution.py:127
  266.9 0.4 slice.18
  267.2 0.3 convolution_add_fusion.1
  267.5 50.3 %all-to-all-done.2 = bf16[64,64,256]{2,1,0:T(8,128)(2,1)} async-done(((bf16[64,64,256]{2,1,0:T(8,128)(2,1)}), bf16[64,64,256]{2,1,0:T(8,128)(2,1)}, u32[]{:S(2)}, u32[]{:S(2)}) %all-to-all-start.2) | async-done | bytes 2097184 | tf_op jit(solution)/shard_map/all_to_all | solution.py:127
  317.8 3.5 convert_select_fusion
  321.3 23.3 %scatter_fusion = f32[512,256]{1,0:T(8,128)S(1)} fusion(f32[512,256]{1,0:T(8,128)S(1)} %convolution_add_fusion.1, s32[4096]{0:T(1024)S(1)} %reshape.164, f32[4096,256]{1,0:T(8,128)} %bitcast.90), kind=kCustom, calls=%fused_computation.4 | custom fusion | flops 1048576 | bytes 12599296 | tf_op jit(solution)/shard_map/scatter-add | solution.py:132
  344.6 0.4 fusion.20
  345.0 1.8 collective-permute-start
  346.8 6.6 %collective-permute-done = bf16[512,256]{1,0:T(8,128)(2,1)S(1)} collective-permute-done((bf16[512,256]{1,0:T(8,128)(2,1)S(1)}, bf16[512,256]{1,0:T(8,128)(2,1)S(1)}, u32[]{:S(2)}, u32[]{:S(2)}) %collective-permute-start) | collective-permute-done | bytes 262176 | tf_op jit(solution)/shard_map/ppermute | solution.py:15
  353.4 1.7 collective-permute-start.1
  355.1 0.9 fusion.38
  356.0 0.9 fusion.37
  356.8 1.1 collective-permute-start.2
  357.9 4.0 collective-permute-done.1
  362.0 2.1 collective-permute-done.2
  364.2 0.3 convolution_bitcast_fusion.2
  364.5 0.3 convolution_bitcast_fusion.1
  364.8 0.7 pad_maximum_fusion.1
  365.6 0.6 subtract_reduce_fusion
  366.2 124.8 %psum.36 = f32[]{:T(128)} all-reduce(f32[]{:T(128)} %subtract_reduce_fusion), channel_id=1, replica_groups=mesh['node'=64,'feat'=4] {'node'}, use_global_device_ids=true, to_apply=%region_6.7 | all-reduce | flops 1 | bytes 8 | tf_op jit(solution)/shard_map/psum | solution.py:113
  491.6 54.8 %all-reduce.6.cloned.1.call-done = (f32[2,32,1024]{2,1,0:T(8,128)}, f32[256,172]{0,1:T(8,128)}, f32[256,172]{0,1:T(8,128)}) async-done(((f32[2,32,1024]{2,1,0:T(8,128)}, f32[256,172]{0,1:T(8,128)}, f32[256,172]{0,1:T(8,128)}), (f32[2,32,1024]{2,1,0:T(8,128)}, f32[256,172]{0,1:T(8,128)}, f32[256,172]{0,1:T(8,128)})) %all-reduce.6.cloned.1.call-update) | async-done | bytes 614416 | tf_op jit(solution)/shard_map/psum | solution.py:144
  546.5 1.7 slice_bitcast_fusion
  548.1 1.6 copy.71
  549.7 1.6 copy.72
  (49 shorter events, 0.8 us)
Async XLA Ops:
  7.2 44.1 %copy-start = (bf16[4,16,128,128]{3,2,1,0:T(8,128)(2,1)S(1)}, bf16[4,16,128,128]{3,2,1,0:T(8,128)(2,1)}, u32[]{:S(2)}) copy-start(bf16[4,16,128,128]{3,2,1,0:T(8,128)(2,1)} %param.14) | copy-start | bytes 6291460
  22.1 15.5 %copy-start.11 = (s32[4,16]{1,0:T(4,128)S(1)}, s32[4,16]{1,0:T(4,128)}, u32[]{:S(2)}) copy-start(s32[4,16]{1,0:T(4,128)} %param.13) | copy-start | bytes 772
  22.1 15.6 %copy-start.5 = (bf16[512,32]{0,1:T(8,128)(2,1)S(1)}, bf16[512,32]{0,1:T(8,128)(2,1)}, u32[]{:S(2)}) copy-start(bf16[512,32]{0,1:T(8,128)(2,1)} %param.10) | copy-start | bytes 98308
  22.1 15.6 %copy-start.10 = (bf16[32,1024]{1,0:T(8,128)(2,1)S(1)}, bf16[32,1024]{1,0:T(8,128)(2,1)}, u32[]{:S(2)}) copy-start(bf16[32,1024]{1,0:T(8,128)(2,1)} %param.16) | copy-start | bytes 196612
  25.4 24.1 %all-to-all-start = ((bf16[64,2,1024]{2,1,0:T(2,128)(2,1)}), bf16[64,2,1024]{2,1,0:T(2,128)(2,1)S(1)}, u32[]{:S(2)}, u32[]{:S(2)}) async-start(bf16[64,2,1024]{2,1,0:T(2,128)(2,1)} %reshape.178), calls=%async_computation | async-start | bytes 524288 | tf_op jit(solution)/shard_map/all_to_all | solution.py:94
  37.5 45.1 %reduce-scatter.2.cloned.1.call-start = ((), (), s32[]{:S(2)}) async-start(), calls=%async_computation.4 | async-start | bytes 2621440 | tf_op jit(solution)/shard_map/reduce_scatter | solution.py:100
  51.3 1.6 copy-start.3
  51.3 1.6 copy-start.9
  105.2 10.9 %copy-start.7 = (bf16[256,172]{0,1:T(8,128)(2,1)S(1)}, bf16[256,172]{0,1:T(8,128)(2,1)}, u32[]{:S(2)}) copy-start(bf16[256,172]{0,1:T(8,128)(2,1)} %param.18) | copy-start | bytes 264196
  105.2 61.9 %all-to-all-start.1 = ((bf16[64,64,256]{2,1,0:T(8,128)(2,1)}), bf16[64,64,256]{2,1,0:T(8,128)(2,1)}, u32[]{:S(2)}, u32[]{:S(2)}) async-start(bf16[64,64,256]{2,1,0:T(8,128)(2,1)} %select_select_fusion), calls=%async_computation.2 | async-start | bytes 4194304 | tf_op jit(solution)/shard_map/all_to_all | solution.py:105
  116.1 105.6 %all-reduce.4.cloned.1.call-start = ((), (), s32[]{:S(2)}) async-start(), calls=%async_computation.5 | async-start | bytes 720896 | tf_op jit(solution)/shard_map/psum | solution.py:111
  174.7 3.2 copy-start.6
  174.7 48.0 %copy-start.12 = (s32[512]{0:T(512)S(1)}, s32[512]{0:T(512)}, u32[]{:S(2)}) copy-start(s32[512]{0:T(512)} %param.15) | copy-start | bytes 6148
  250.8 2.3 copy-start.2
  255.9 10.9 %copy-start.8 = (s32[1,64,64]{2,1,0:T(8,128)S(1)}, s32[1,64,64]{2,1,0:T(8,128)}, u32[]{:S(2)}) copy-start(s32[1,64,64]{2,1,0:T(8,128)} %param.11) | copy-start | bytes 49156
  255.9 11.0 %slice-start = ((f32[36,32768]{1,0:T(8,128)}), f32[4,32768]{1,0:T(4,128)S(1)}, s32[]{:S(2)}) async-start(f32[36,32768]{1,0:T(8,128)} %copy-done.2), calls=%async_computation.7 | async-start | bytes 1048576 | tf_op jit(solution)/shard_map/slice | solution.py:135
  255.9 61.9 %all-to-all-start.2 = ((bf16[64,64,256]{2,1,0:T(8,128)(2,1)}), bf16[64,64,256]{2,1,0:T(8,128)(2,1)}, u32[]{:S(2)}, u32[]{:S(2)}) async-start(bf16[64,64,256]{2,1,0:T(8,128)(2,1)} %convert_element_type.51), calls=%async_computation.3 | async-start | bytes 4194304 | tf_op jit(solution)/shard_map/all_to_all | solution.py:127
  266.7 279.7 %all-reduce.6.cloned.1.call-start = ((), (), s32[]{:S(2)}) async-start(), calls=%async_computation.6 | async-start | bytes 1245184 | tf_op jit(solution)/shard_map/psum | solution.py:144
  321.3 23.3 %copy-start.4 = (f32[512,256]{1,0:T(8,128)S(1)}, f32[512,256]{1,0:T(8,128)}, u32[]{:S(2)}) copy-start(f32[512,256]{1,0:T(8,128)} %reduce-scatter.2.cloned.1.call-done) | copy-start | bytes 1572868
  345.0 8.4 %collective-permute-start = (bf16[512,256]{1,0:T(8,128)(2,1)S(1)}, bf16[512,256]{1,0:T(8,128)(2,1)S(1)}, u32[]{:S(2)}, u32[]{:S(2)}) collective-permute-start(bf16[512,256]{1,0:T(8,128)(2,1)S(1)} %fusion.20), channel_id=1, source_target_pairs={{0,1},{1,2},{2,3},{3,0},{4,5},{5,6},{6,7},{7,4},{8,9},{9,10},{10,1... | collective-permute-start | bytes 786440 | tf_op jit(solution)/shard_map/ppermute | solution.py:15
  353.4 8.5 %collective-permute-start.1 = (bf16[512,256]{1,0:T(8,128)(2,1)S(1)}, bf16[512,256]{1,0:T(8,128)(2,1)S(1)}, u32[]{:S(2)}, u32[]{:S(2)}) collective-permute-start(bf16[512,256]{1,0:T(8,128)(2,1)S(1)} %collective-permute-done), channel_id=1, source_target_pairs={{0,1},{1,2},{2,3},{3,0},{4,5},{5,6},{6,7},{7,4},{8,9},{9,10},{10,1... | collective-permute-start | bytes 786440 | tf_op jit(solution)/shard_map/ppermute | solution.py:15
  356.8 7.2 %collective-permute-start.2 = (bf16[512,256]{1,0:T(8,128)(2,1)S(1)}, bf16[512,256]{1,0:T(8,128)(2,1)S(1)}, u32[]{:S(2)}, u32[]{:S(2)}) collective-permute-start(bf16[512,256]{1,0:T(8,128)(2,1)S(1)} %fusion.20), channel_id=1, source_target_pairs={{0,3},{1,0},{2,1},{3,2},{4,7},{5,4},{6,5},{7,6},{8,11},{9,8},{10,9... | collective-permute-start | bytes 786440 | tf_op jit(solution)/shard_map/ppermute | solution.py:17
  364.2 187.1 %copy-start.1 = (bf16[4,16,128,128]{3,2,1,0:T(8,128)(2,1)S(1)}, bf16[4,16,128,128]{3,2,1,0:T(8,128)(2,1)}, u32[]{:S(2)}) copy-start(bf16[4,16,128,128]{3,2,1,0:T(8,128)(2,1)} %param.14) | copy-start | bytes 6291460
Sparse Core Ops, SparseCore 0:
  54.8 27.8 reduce-scatter.1
  179.1 42.5 all-reduce.3
  365.7 180.7 all-reduce.5
